TPU v7x, 32 devices: a whole 2x2x4 slice. The times are simulated.
32 devices in a mesh: row: 4 (over z), col: 4 (over x, core), grp: 2 (over y).
Axes of the slice: x: 2, y: 2, z: 4, core: 2. Of those that a mesh axis runs over, the one named last changes fastest.
Arguments:
- matrix: float32 [16384, 16384], P('row', ('col', 'grp')), may hold values from -8 to 8, as said below
- basis_rows: float32 [4096, 16384], P(('col', 'grp'), 'row'), may hold values from -6 to 6
- reflectors: float32 [16384, 512], P('row'), may hold values from -0.125 to 0.125
- tfactor: float32 [512, 512], replicated, may hold values from -0.25 to 2, as said below
Outputs:
- new_matrix: float32 [16384, 16384], P('row', ('col', 'grp'))
- new_basis: float32 [4096, 16384], P(('col', 'grp'), 'row')
Inputs may be any that keep to these rules, and one draw needn't show every extreme that they name: The matrix A that it represents is symmetric. `tfactor`: upper triangular: zero below the diagonal, diagonal between 1 and 2.
All inputs are finite; a program needn't handle non-finite values.
Results may differ from a plain program's by a relative error of at most 0.000073.
Values sent between devices are 32-bit elements; how exact they have to be, the bound alone decides.
A program may use at most 192 MiB of HBM per device.

v0:
```python
import jax
import jax.numpy as jnp
from jax import lax
from jax.experimental import pallas as pl
from jax.experimental.pallas import tpu as pltpu
from jax.sharding import PartitionSpec as P


def halves(x):
    high = x.astype(jnp.bfloat16)
    return high, (x - high.astype(jnp.float32)).astype(jnp.bfloat16)


def apply_kernel(index_ref, a_ref, v_ref, *rest):
    out_ref = rest[-1]
    a_high, a_low = halves(a_ref[...])
    v_high, v_low = halves(v_ref[...])
    product = jnp.dot(
        jnp.concatenate([a_high, a_low, a_high], axis=1),
        jnp.concatenate([v_high, v_high, v_low], axis=0),
        preferred_element_type=jnp.float32,
    )
    out_ref[...] = product if len(rest) == 1 else rest[0][...] + product


def apply_chunk(matrix, chunk, total, index):
    rows, (depth, wide) = matrix.shape[0], chunk.shape
    tile = min(512, rows)
    specs = [
        pl.BlockSpec((tile, depth), lambda i, c: (i, c[0])),
        pl.BlockSpec((depth, wide), lambda i, c: (0, 0)),
    ]
    args = [matrix, chunk]
    if total is not None:
        specs.append(pl.BlockSpec((tile, wide), lambda i, c: (i, 0)))
        args.append(total)
    return pl.pallas_call(
        apply_kernel,
        out_shape=jax.ShapeDtypeStruct((rows, wide), jnp.float32),
        grid_spec=pltpu.PrefetchScalarGridSpec(
            num_scalar_prefetch=1,
            grid=(rows // tile,),
            in_specs=specs,
            out_specs=pl.BlockSpec((tile, wide), lambda i, c: (i, 0)),
        ),
        cost_estimate=pl.CostEstimate(
            flops=6 * rows * depth * wide,
            bytes_accessed=4 * rows * (depth + 2 * wide),
            transcendentals=0,
        ),
        name="apply_chunk",
    )(index, *args)


def update_kernel(order_ref, a_ref, near_ref, far_ref, vr_ref, vc_ref, zc_ref, *rest):
    out_ref, right = rest[-2:]

    @pl.when(pl.program_id(0) == 0)
    def _():
        v_high, v_low = halves(vc_ref[...])
        z_high, z_low = halves(zc_ref[...])
        right[...] = jnp.concatenate([v_high, v_high, v_low, z_high, z_high, z_low], axis=1)

    first = pl.program_id(0) < pl.num_programs(0) // 2
    w_high, w_low = halves(jnp.where(first, near_ref[...], far_ref[...]))
    v_high, v_low = halves(vr_ref[...])
    left = jnp.concatenate([w_high, w_low, w_high, v_high, v_low, v_high], axis=1)
    out_ref[...] = a_ref[...] - lax.dot_general(
        left, right[...], (((1,), (1,)), ((), ())), preferred_element_type=jnp.float32
    )


def update_chunk(matrix, w_near, w_far, v_row, v_chunk, z_chunk, order, out):
    rows, (depth, wide) = matrix.shape[0], v_chunk.shape
    steps = order.shape[0] - 1
    tile, half = rows // steps, steps // 2
    specs = [
        pl.BlockSpec((tile, depth), lambda i, c: (c[i + 1], c[0])),
        pl.BlockSpec((tile, wide), lambda i, c: (jnp.minimum(i, half - 1), 0)),
        pl.BlockSpec((tile, wide), lambda i, c: (jnp.maximum(i - half, 0), 0)),
        pl.BlockSpec((tile, wide), lambda i, c: (c[i + 1], 0)),
        pl.BlockSpec((depth, wide), lambda i, c: (0, 0)),
        pl.BlockSpec((depth, wide), lambda i, c: (0, 0)),
    ]
    args = [matrix, w_near, w_far, v_row, v_chunk, z_chunk]
    alias = {}
    if out is not None:
        specs.append(pl.BlockSpec(memory_space=pl.ANY))
        args.append(out)
        alias = {7: 0}
    return pl.pallas_call(
        update_kernel,
        out_shape=jax.ShapeDtypeStruct(matrix.shape, jnp.float32),
        grid_spec=pltpu.PrefetchScalarGridSpec(
            num_scalar_prefetch=1,
            grid=(steps,),
            in_specs=specs,
            out_specs=pl.BlockSpec((tile, depth), lambda i, c: (c[i + 1], c[0])),
            scratch_shapes=[pltpu.VMEM((depth, 6 * wide), jnp.bfloat16)],
        ),
        input_output_aliases=alias,
        cost_estimate=pl.CostEstimate(
            flops=12 * rows * depth * wide,
            bytes_accessed=8 * rows * (depth + wide),
            transcendentals=0,
        ),
        name="update_chunk",
    )(order, *args)


def dot(a, b):
    return jnp.dot(a, b, precision=lax.Precision.HIGH, preferred_element_type=jnp.float32)


def swap(x, axis, bit):
    count = lax.axis_size(axis)
    return lax.ppermute(x, axis, [(i, i ^ bit) for i in range(count)])


def pick(x, index, axis):
    return lax.dynamic_index_in_dim(x, index, axis, keepdims=False)


def scatter_sum(total):
    if lax.axis_size("col") != 4 or lax.axis_size("grp") != 2:
        return lax.psum_scatter(total, ("col", "grp"), scatter_dimension=0, tiled=True)
    col, y = lax.axis_index("col"), lax.axis_index("grp")
    x, core = col // 2, col % 2
    depth, wide = total.shape[0] // 8, total.shape[1]
    total = total.reshape(2, 2, 2, depth, wide)
    mine = pick(total, core, 1) + swap(pick(total, 1 - core, 1), "col", 1)
    near, far = mine[:, :, : depth // 2], mine[:, :, depth // 2 :]
    near_in = swap(pick(near, 1 - x, 0), "col", 2)
    far_in = swap(pick(far, 1 - y, 1), "grp", 1)
    near = pick(near, x, 0) + near_in
    far = pick(far, y, 1) + far_in
    near_in = swap(pick(near, 1 - y, 0), "grp", 1)
    far_in = swap(pick(far, 1 - x, 0), "col", 2)
    return jnp.concatenate([pick(near, y, 0) + near_in, pick(far, x, 0) + far_in], axis=0)


def gather_rows(own):
    if lax.axis_size("col") != 4 or lax.axis_size("grp") != 2:
        whole = lax.all_gather(own, ("col", "grp"), axis=0, tiled=True)
        half = whole.shape[0] // 2
        tiles = jnp.arange(whole.shape[0] // own.shape[0])
        return whole[:half], whole[half:], tiles
    depth, _ = own.shape
    near, far = own[None, : depth // 2], own[None, depth // 2 :]
    near = jnp.concatenate([near, swap(near, "grp", 1)])
    far = jnp.concatenate([far, swap(far, "col", 2)])
    near_in, far_in = swap(near, "col", 2), swap(far, "grp", 1)
    near = jnp.concatenate([near, near_in])
    tiles = []
    for tile in range(4):
        source, place = (far, far_in)[tile % 2], tile // 2
        tiles += [near[tile], source[place]]
    mine = jnp.concatenate(tiles, axis=0)
    col, y = lax.axis_index("col"), lax.axis_index("grp")
    bits = jnp.arange(8)
    cols = col ^ (2 * (bits // 2 % 2) + bits // 4)
    rest = swap(mine, "col", 1)
    return mine, rest, cols * 2 + (y ^ (bits % 2))


def ring_step(matrix, basis_rows, reflectors, tfactor):
    plane = ("col", "grp")
    member, groups = lax.axis_index(plane), lax.axis_size(plane)
    row, count = lax.axis_index("row"), lax.axis_size("row")
    ring = [(i, (i + 1) % count) for i in range(count)]
    slice_rows = reflectors.shape[0] // groups
    own_v = lax.dynamic_slice_in_dim(reflectors, member * slice_rows, slice_rows, 0)

    v_chunks, owners = [own_v], []
    for step in range(count):
        owners.append(((row - step + count) % count).astype(jnp.int32).reshape(1))
        if step + 1 < count:
            v_chunks.append(lax.ppermute(v_chunks[-1], "row", ring))
    total = apply_chunk(matrix, own_v, None, owners[0])
    total, q_proj = lax.optimization_barrier((total, dot(basis_rows, reflectors)))
    q_proj = lax.psum(q_proj, "row")
    for chunk, owner in zip(v_chunks[1:], owners[1:]):
        total = apply_chunk(matrix, chunk, total, owner)

    cross, total = lax.optimization_barrier((dot(reflectors.T, total), total))
    cross = lax.psum_scatter(cross, plane, scatter_dimension=0, tiled=True)
    applied = scatter_sum(total)
    w_slice = dot(applied, tfactor)
    cross, w_slice = lax.optimization_barrier((cross, w_slice))
    cross = lax.all_gather(lax.psum(cross, "row"), plane, axis=0, tiled=True)
    w_chunks = [w_slice]
    for _ in range(count - 1):
        w_chunks.append(lax.ppermute(w_chunks[-1], "row", ring))
    w_near, w_far, tiles = gather_rows(w_slice)
    inner = dot(tfactor.T, dot(cross, tfactor))

    out = None
    for v_chunk, w_chunk, owner in zip(v_chunks, w_chunks, owners):
        if out is not None:
            out, w_chunk = lax.optimization_barrier((out, w_chunk))
        z_chunk = w_chunk - dot(v_chunk, inner.T)
        order = jnp.concatenate([owner, tiles.astype(jnp.int32)])
        out = update_chunk(matrix, w_near, w_far, reflectors, v_chunk, z_chunk, order, out)

    new_basis = basis_rows - dot(dot(q_proj, tfactor), reflectors.T)
    return (out, new_basis)


MESH = pl.DeviceIdType.MESH
INNER, FINAL, OUTER = [(1, 2), (2, 1)], [(2, 3), (1, 0)], [(0, 1), (3, 2)]


def triple(a, b, dims):
    a_high, a_low = halves(a)
    b_high, b_low = halves(b)
    (left,), (right,) = dims
    return lax.dot_general(
        jnp.concatenate([a_high, a_low, a_high], axis=left),
        jnp.concatenate([b_high, b_high, b_low], axis=right),
        (dims, ((), ())),
        preferred_element_type=jnp.float32,
    )


def front_kernel(
    a_hbm, v_hbm, own_hbm, b_hbm, t_ref,
    v_all, w_all, w_rows, q_out, cross_out,
    a_buf, b_buf, v_buf, own, part, outer_in, inner_in, final_in, w_own, q_acc, total,
    half_in, quarter_in, eighth_in, line_in, far_in,
    a_sem, b_sem, v_sem, local_sem, send_sem, recv_sem,
):
    z, col, y = (lax.axis_index(name) for name in ("row", "col", "grp"))
    core, x = lax.rem(col, 2), lax.div(col, 2)
    depth = own.shape[0]
    tile = a_buf.shape[1]
    steps = v_buf.shape[0] // tile
    low = z < 2
    edge = (z == 0) | (z == 3)
    near = jnp.where(low, 1, 2)
    outward = jnp.where(low, 0, 3)
    across = jnp.where(low, 2, 1)
    beside = z + 1 - 2 * lax.rem(z, 2)
    dests = [jnp.where(low, 3, 0), jnp.where(low, 2, 1), beside, z]
    partner = {"row": z, "col": col, "grp": y}
    by_core = partner | {"col": col + 1 - 2 * core}
    by_x = partner | {"col": core + 2 * (1 - x)}
    by_y = partner | {"grp": 1 - y}

    def along(where):
        return partner | {"row": where}

    barrier = pltpu.get_barrier_semaphore()
    for target in (by_core, by_x, by_y, along(lax.rem(z + 1, 4)), along(lax.rem(z + 2, 4)), along(lax.rem(z + 3, 4))):
        pl.semaphore_signal(barrier, inc=1, device_id=target, device_id_type=MESH)
    pl.semaphore_wait(barrier, 6)

    def remote(slot, source, target_ref, target):
        return pltpu.make_async_remote_copy(
            src_ref=source, dst_ref=target_ref, send_sem=send_sem.at[slot], recv_sem=recv_sem.at[slot],
            device_id=target, device_id_type=MESH,
        )

    def spread(base, source, slots):
        return {
            "in": remote(base, source, slots.at[1], along(near)),
            "out": remote(base + 1, source, slots.at[0], along(outward)),
            "over": remote(base + 2, source, slots.at[0], along(across)),
            "out2": remote(base + 3, slots.at[0], slots.at[1], along(outward)),
            "over2": remote(base + 4, slots.at[1], slots.at[2], along(across)),
            "out3": remote(base + 5, slots.at[2], slots.at[2], along(outward)),
        }

    def fetch_a(index, step, slot):
        columns = pl.ds(pl.multiple_of(index * depth, depth), depth)
        rows = pl.ds(pl.multiple_of(step * tile, tile), tile)
        return pltpu.make_async_copy(a_hbm.at[rows, columns], a_buf.at[slot], a_sem.at[slot])

    def fetch_b(step, slot):
        columns = pl.ds(pl.multiple_of(step * tile, tile), tile)
        return pltpu.make_async_copy(b_hbm.at[:, columns], b_buf.at[slot], b_sem.at[slot])

    def fetch_v(step):
        rows = pl.ds(pl.multiple_of(step * tile, tile), tile)
        return pltpu.make_async_copy(v_hbm.at[rows, :], v_buf.at[rows, :], v_sem.at[step])

    gather_v = spread(0, own_hbm, v_all)
    gather_w = spread(6, w_own, w_all)

    @pl.when(edge)
    def _():
        gather_v["in"].start()

    @pl.when(jnp.logical_not(edge))
    def _():
        gather_v["over"].start()
        gather_v["out"].start()

    fetch_a(dests[0], 0, 0).start()
    fetch_v(0).start()
    for step in range(1, steps):
        fetch_v(step).start()
    fetch_own = pltpu.make_async_copy(own_hbm, own, local_sem.at[0])
    fetch_own.start()

    outer = [remote(12 + i, part.at[i], outer_in.at[i], along(near)) for i in range(3)]
    inner = [remote(15 + i, outer_in.at[i], inner_in.at[i], along(across)) for i in range(2)]
    final = remote(17, inner_in.at[0], final_in, along(outward))

    def product(i):
        def body(step, carry):
            slot = lax.rem(step, 2)
            if i == 0:
                fetch_v(step).wait()
            following = dests[i + 1] if i < 3 else dests[i]
            index = jnp.where(step < steps - 1, dests[i], following)
            ahead = lax.rem(step + 1, steps)
            if i < 3:
                fetch_a(index, ahead, 1 - slot).start()
            else:
                @pl.when(step < steps - 1)
                def _():
                    fetch_a(index, ahead, 1 - slot).start()
            fetch_a(dests[i], step, slot).wait()
            rows = pl.ds(pl.multiple_of(step * tile, tile), tile)
            value = triple(a_buf[slot], v_buf[rows, :], ((0,), (0,)))

            @pl.when(step == 0)
            def _():
                part[i] = value

            @pl.when(step > 0)
            def _():
                part[i] += value

            return carry

        lax.fori_loop(0, steps, body, 0)

    for i in range(3):
        product(i)

        @pl.when(edge)
        def _():
            outer[i].start()

        if i == 1:
            @pl.when(jnp.logical_not(edge))
            def _():
                gather_v["over"].wait_recv()
                gather_v["out2"].start()
                gather_v["in"].wait_recv()
                gather_v["over2"].start()

    @pl.when(jnp.logical_not(edge))
    def _():
        outer[0].wait_recv()
        outer_in[0] += part[0]
        inner[0].start()

    fetch_b(0, 0).start()
    product(3)

    @pl.when(jnp.logical_not(edge))
    def _():
        gather_v["over2"].wait_recv()
        gather_v["out3"].start()
        outer[1].wait_recv()
        outer_in[1] += part[1]
        inner[1].start()

    def project_b(step, carry):
        slot = lax.rem(step, 2)

        @pl.when(step < steps - 1)
        def _():
            fetch_b(step + 1, 1 - slot).start()

        fetch_b(step, slot).wait()
        rows = pl.ds(pl.multiple_of(step * tile, tile), tile)
        value = triple(b_buf[slot], v_buf[rows, :], ((1,), (0,)))

        @pl.when(step == 0)
        def _():
            q_acc[...] = value

        @pl.when(step > 0)
        def _():
            q_acc[...] += value

        return carry

    @pl.when(jnp.logical_not(edge))
    def _():
        inner[0].wait_recv()
        inner_in[0] += part[2]
        final.start()

    lax.fori_loop(0, steps, project_b, 0)
    put_q = pltpu.make_async_copy(q_acc, q_out, local_sem.at[1])
    put_q.start()

    @pl.when(jnp.logical_not(edge))
    def _():
        inner[1].wait_recv()
        part[3] += inner_in[1]
        outer[2].wait_recv()
        part[3] += outer_in[2]

    @pl.when(edge)
    def _():
        final.wait_recv()
        part[3] += final_in[...]

    w_own[...] = triple(part[3], t_ref[...], ((1,), (0,)))

    half = depth // 2
    places = [pl.ds(i * depth, half) for i in range(8)], [pl.ds(i * depth + half, half) for i in range(8)]
    top, bottom = pl.ds(0, half), pl.ds(half, half)
    hops = [
        remote(18, w_own.at[top], w_rows.at[places[0][1]], by_y),
        remote(19, w_own.at[bottom], w_rows.at[places[1][2]], by_x),
        remote(20, w_own.at[top], w_rows.at[places[0][2]], by_x),
        remote(21, w_own.at[bottom], w_rows.at[places[1][1]], by_y),
        remote(22, w_rows.at[places[0][1]], w_rows.at[places[0][3]], by_x),
        remote(23, w_rows.at[places[1][2]], w_rows.at[places[1][3]], by_y),
    ]
    shares = [remote(24, w_own, w_rows.at[pl.ds(4 * depth, depth)], by_core)]
    for slot, (side, i) in enumerate([(0, 1), (1, 2), (0, 2), (1, 1), (0, 3), (1, 3)]):
        shares.append(remote(25 + slot, w_rows.at[places[side][i]], w_rows.at[places[side][4 + i]], by_core))

    for hop in hops[:2]:
        hop.start()

    total[...] = triple(own_value(fetch_own, own), part[3], ((0,), (0,)))

    def piece(start, size):
        return pl.ds(pl.multiple_of(start, size), size)

    sizes = [depth // 2, depth // 4, depth // 8]
    bits, targets, landings = [core, x, y], [by_core, by_x, by_y], [half_in, quarter_in, eighth_in]
    base = 0
    reduces = []
    for i in range(3):
        other = base + (1 - bits[i]) * sizes[i]
        base = base + bits[i] * sizes[i]
        copy = remote(31 + i, total.at[piece(other, sizes[i])], landings[i], targets[i])
        copy.start()
        copy.wait_recv()
        here = piece(base, sizes[i])
        total[here, :] += landings[i][...]
        reduces.append(copy)
    mine = piece(base, sizes[2])
    line = [
        remote(34, total.at[mine], line_in, along(beside)),
        remote(35, eighth_in, far_in, along(lax.rem(z + 2, 4))),
    ]
    line[0].start()

    @pl.when(edge)
    def _():
        gather_w["in"].start()

    @pl.when(jnp.logical_not(edge))
    def _():
        gather_w["over"].start()
        gather_w["out"].start()

    shares[0].start()
    hops[2].start()
    hops[3].start()
    put_w = pltpu.make_async_copy(w_own, w_rows.at[pl.ds(0, depth)], local_sem.at[2])
    put_w.start()

    line[0].wait()
    eighth_in[...] = total[mine, :] + line_in[...]
    line[1].start()

    for i in range(2):
        hops[i].wait_recv()
        hops[4 + i].start()
        shares[1 + i].start()

    line[1].wait()
    eighth_in[...] += far_in[...]
    put_c = pltpu.make_async_copy(eighth_in, cross_out.at[mine], local_sem.at[3])
    put_c.start()
    put_c.wait()
    returns = []
    for i in (2, 1, 0):
        here = piece(base - lax.rem(base, sizes[i]), sizes[i])
        copy = remote(36 + i, cross_out.at[here], cross_out.at[here], targets[i])
        copy.start()
        copy.wait_recv()
        returns.append(copy)

    @pl.when(jnp.logical_not(edge))
    def _():
        gather_w["over"].wait_recv()
        gather_w["out2"].start()
        gather_w["in"].wait_recv()
        gather_w["over2"].start()

    for i in range(2, 6):
        hops[i].wait_recv()
        shares[1 + i].start()
    for copy in hops + shares + reduces + returns:
        copy.wait_send()
    for copy in shares:
        copy.wait_recv()
    put_w.wait()
    put_q.wait()

    @pl.when(edge)
    def _():
        gather_v["in"].wait_send()
        gather_w["in"].wait_send()
        for copy in outer:
            copy.wait_send()
        for name in ("out", "out2", "out3"):
            gather_v[name].wait_recv()
        for name in ("out", "out2"):
            gather_w[name].wait_recv()

    @pl.when(jnp.logical_not(edge))
    def _():
        for name in ("over", "out", "out2", "over2", "out3"):
            gather_v[name].wait_send()
        for name in ("over", "out", "out2", "over2"):
            gather_w[name].wait_send()
        for copy in inner + [final]:
            copy.wait_send()
        gather_w["over2"].wait_recv()


def own_value(fetch, own):
    fetch.wait()
    return own[...]


def front(matrix, reflectors, own_v, basis_rows, tfactor):
    depth, wide = own_v.shape
    rows = reflectors.shape[0]
    tile = rows // 4
    hbm = pl.BlockSpec(memory_space=pltpu.HBM)
    chunk = (depth, wide)

    def shape(*dims):
        return jax.ShapeDtypeStruct(dims, jnp.float32)

    def vmem(*dims):
        return pltpu.VMEM(dims, jnp.float32)

    return pl.pallas_call(
        front_kernel,
        out_shape=[shape(3, *chunk), shape(3, *chunk), shape(8 * depth, wide), shape(*chunk), shape(*chunk)],
        in_specs=[hbm] * 4 + [pl.BlockSpec(memory_space=pltpu.VMEM)],
        out_specs=[hbm] * 5,
        scratch_shapes=[
            vmem(2, tile, depth), vmem(2, depth, tile), vmem(rows, wide), vmem(*chunk), vmem(4, *chunk),
            vmem(3, *chunk), vmem(2, *chunk), vmem(*chunk), vmem(*chunk), vmem(*chunk), vmem(*chunk),
            vmem(depth // 2, wide), vmem(depth // 4, wide), vmem(depth // 8, wide), vmem(depth // 8, wide),
            vmem(depth // 8, wide),
            pltpu.SemaphoreType.DMA((2,)), pltpu.SemaphoreType.DMA((2,)), pltpu.SemaphoreType.DMA((4,)),
            pltpu.SemaphoreType.DMA((4,)), pltpu.SemaphoreType.DMA((39,)), pltpu.SemaphoreType.DMA((39,)),
        ],
        compiler_params=pltpu.CompilerParams(
            collective_id=0, has_side_effects=True, vmem_limit_bytes=60 * 1024 * 1024
        ),
        cost_estimate=pl.CostEstimate(
            flops=30 * rows * depth * wide, bytes_accessed=20 * rows * depth, transcendentals=0
        ),
        name="front",
    )(matrix, reflectors, own_v, basis_rows, tfactor)


def finish_kernel(order_ref, a_ref, w_ref, v_ref, vc_ref, wc_ref, y_ref, *rest):
    out_ref, right = rest[-2:]

    @pl.when(pl.program_id(0) == 0)
    def _():
        chunk = vc_ref[...]
        z_high, z_low = halves(wc_ref[...] - triple(chunk, y_ref[...], ((1,), (1,))))
        v_high, v_low = halves(chunk)
        right[...] = jnp.concatenate([v_high, v_high, v_low, z_high, z_high, z_low], axis=1)

    w_high, w_low = halves(w_ref[...])
    v_high, v_low = halves(v_ref[...])
    left = jnp.concatenate([w_high, w_low, w_high, v_high, v_low, v_high], axis=1)
    out_ref[...] = a_ref[...] - lax.dot_general(
        left, right[...], (((1,), (1,)), ((), ())), preferred_element_type=jnp.float32
    )


def finish_chunk(matrix, w_rows, v_row, v_chunks, w_chunks, slots, inner, order, out):
    rows, (depth, wide) = matrix.shape[0], v_chunks.shape[1:]
    tile, steps = depth, rows // depth
    specs = [
        pl.BlockSpec((tile, depth), lambda i, c: (c[i + 1], c[0])),
        pl.BlockSpec((tile, wide), lambda i, c: (i, 0)),
        pl.BlockSpec((tile, wide), lambda i, c: (c[i + 1], 0)),
        pl.BlockSpec((None, depth, wide), lambda i, c: (slots[0], 0, 0)),
        pl.BlockSpec((None, depth, wide), lambda i, c: (slots[1], 0, 0)),
        pl.BlockSpec(inner.shape, lambda i, c: (0, 0)),
    ]
    args = [matrix, w_rows, v_row, v_chunks, w_chunks, inner]
    alias = {}
    if out is not None:
        specs.append(pl.BlockSpec(memory_space=pl.ANY))
        args.append(out)
        alias = {7: 0}
    return pl.pallas_call(
        finish_kernel,
        out_shape=jax.ShapeDtypeStruct(matrix.shape, jnp.float32),
        grid_spec=pltpu.PrefetchScalarGridSpec(
            num_scalar_prefetch=1,
            grid=(steps,),
            in_specs=specs,
            out_specs=pl.BlockSpec((tile, depth), lambda i, c: (c[i + 1], c[0])),
            scratch_shapes=[pltpu.VMEM((depth, 6 * wide), jnp.bfloat16)],
        ),
        input_output_aliases=alias,
        cost_estimate=pl.CostEstimate(
            flops=12 * rows * depth * wide,
            bytes_accessed=8 * rows * (depth + wide),
            transcendentals=0,
        ),
        name="finish_chunk",
    )(order, *args)


def scalar(x):
    return x.astype(jnp.int32).reshape(1)


def send(x, pairs):
    return lax.ppermute(x, "row", pairs)


def line_step(matrix, basis_rows, reflectors, tfactor):
    z, col, y = (lax.axis_index(name) for name in ("row", "col", "grp"))
    member, groups = lax.axis_index(("col", "grp")), lax.axis_size(("col", "grp"))
    depth = reflectors.shape[0] // groups
    own_v = lax.dynamic_slice_in_dim(reflectors, member * depth, depth, 0)
    v_all, w_all, w_rows, q_proj, cross = front(matrix, reflectors, own_v, basis_rows, tfactor)
    inner = dot(tfactor.T, dot(cross, tfactor))

    bits = jnp.arange(8)
    tiles = (col ^ (2 * (bits // 2 % 2) + bits // 4)) * 2 + (y ^ (bits % 2))
    edge, low = (z == 0) | (z == 3), z < 2
    owners = [
        z,
        jnp.where(edge, jnp.where(low, 1, 2), jnp.where(low, 2, 1)),
        jnp.where(edge, jnp.where(low, 2, 1), jnp.where(low, 0, 3)),
        jnp.where(low, 3, 0),
    ]
    w_third = w_all[2]
    w_last = jnp.where(edge, send(w_third, FINAL), w_third)
    q_pair = q_proj + send(q_proj, OUTER)

    out = None
    for i, owner in enumerate(owners):
        order = jnp.concatenate([scalar(owner), tiles.astype(jnp.int32)])
        if i == 2:
            out, q_pair = lax.optimization_barrier((out, q_pair))
            q_full = q_pair + send(q_pair, INNER)
        if i == 3:
            out, q_full, w_last = lax.optimization_barrier((out, q_full, w_last))
            q_full = jnp.where(edge, send(q_full, FINAL), q_full)
        v_from, w_from, slots = v_all, w_all, (i - 1, i - 1)
        if i == 0:
            v_from, w_from, slots = own_v[None], w_rows.reshape(groups, depth, -1), (0, 0)
        if i == 3:
            w_from, slots = w_last[None], (2, 0)
        out = finish_chunk(matrix, w_rows, reflectors, v_from, w_from, slots, inner, order, out)

    out, q_full = lax.optimization_barrier((out, q_full))
    new_basis = basis_rows - dot(dot(q_full, tfactor), reflectors.T)
    return (out, new_basis)


def on_device(*args):
    sizes = tuple(lax.axis_size(name) for name in ("row", "col", "grp"))
    return (line_step if sizes == (4, 4, 2) else ring_step)(*args)


def solution(mesh):
    placed = (P("row", ("col", "grp")), P(("col", "grp"), "row"), P("row", None), P())
    return jax.shard_map(
        on_device,
        mesh=mesh,
        in_specs=placed,
        out_specs=(P("row", ("col", "grp")), P(("col", "grp"), "row")),
        check_vma=False,
    )
```

profile of v0, /device:TPU:0, one launch (start us, length us, event | category | flops | bytes accessed | tf_op | source)
XLA Modules:
  0.0 327.8 jit_solution(11597385957715476130)
XLA Ops:
  0.6 2.3 constant_dynamic-slice_fusion.own_hbm
  2.9 0.0 copy-start
  2.9 189.9 %front.1 = (f32[3,512,512]{2,1,0:T(8,128)}, f32[3,512,512]{2,1,0:T(8,128)}, f32[4096,512]{1,0:T(8,128)}, f32[512,512]{1,0:T(8,128)}, f32[512,512]{1,0:T(8,128)}) custom-call(f32[4096,2048]{1,0:T(8,128)} %a_ref.7, f32[4096,512]{1,0:T(8,128)} %v_ref.7, f32[512,512]{1,0:T(8,128)} %constant_dynamic-slice_fusion.own_hbm, f32[512,4096]{1,0:T(8,128)} %b_hbm.1, ...), custom_call_target="tpu_custom_call" | custom-call | flops 32212254720 | bytes 41943040 | tf_op jit(solution)/shard_map/front/pallas_call | solution.py:553
  192.8 4.4 %collective-permute-start = (f32[512,512]{1,0:T(8,128)}, f32[512,512]{1,0:T(8,128)}, u32[]{:S(2)}, u32[]{:S(2)}) collective-permute-start(f32[512,512]{1,0:T(8,128)} %get-tuple-element.18), channel_id=1, source_target_pairs={{0,8},{24,16},{1,9},{25,17},{2,10},{26,18},{3,11},{27,19},{4,12},{... | collective-permute-start | bytes 3145736 | tf_op jit(solution)/shard_map/ppermute | solution.py:636
  197.2 2.3 slice_bitcast_fusion
  199.4 1.5 collective-permute-start.2
  200.9 2.3 fusion.17.vc_ref
  203.2 0.0 copy-done
  203.2 2.2 fusion.7
  205.5 2.0 convolution_bitcast_fusion.y_ref
  207.5 0.7 pad_add_fusion.3
  208.1 22.0 %finish_chunk.4.rest_0_ = f32[4096,2048]{1,0:T(8,128)} custom-call(s32[9]{0:T(128)} %get-tuple-element.26.order_ref, f32[4096,2048]{1,0:T(8,128)} %a_ref.7, f32[4096,512]{1,0:T(8,128)} %get-tuple-element.14.w_ref, f32[4096,512]{1,0:T(8,128)} %v_ref.7, f32[1,512,512]{2,1,0:T(8,128)} %fusion.17.vc_ref, f32[8,512,512]{2,1,0:T(8,128)} %bitcast.22, ...), custom_call_target="tpu_custom_call" | custom-call | flops 12884901888 | bytes 33554432 | tf_op jit(solution)/shard_map/finish_chunk/pallas_call | solution.py:611
  230.1 0.0 copy-start.1
  230.1 22.1 %finish_chunk.5.rest_0_ = f32[4096,2048]{1,0:T(8,128)} custom-call(s32[9]{0:T(128)} %get-tuple-element.28.order_ref, f32[4096,2048]{1,0:T(8,128)} %a_ref.7, f32[4096,512]{1,0:T(8,128)} %get-tuple-element.14.w_ref, f32[4096,512]{1,0:T(8,128)} %v_ref.7, f32[3,512,512]{2,1,0:T(8,128)} %get-tuple-element.15.vc_ref, ...), custom_call_target="tpu_custom_call", output_to_operand_aliasing={{}: (7, {})} | custom-call | flops 12884901888 | bytes 33554432 | tf_op jit(solution)/shard_map/finish_chunk/pallas_call | solution.py:611
  252.2 0.0 collective-permute-done
  252.2 0.0 copy-done.1
  252.2 1.4 add.36
  253.7 1.7 collective-permute-start.1
  255.3 0.0 collective-permute-done.2
  255.3 2.7 broadcast_select_fusion.1
  258.1 22.0 %finish_chunk.6.rest_0_ = f32[4096,2048]{1,0:T(8,128)} custom-call(s32[9]{0:T(128)} %get-tuple-element.27.order_ref, f32[4096,2048]{1,0:T(8,128)} %a_ref.7, f32[4096,512]{1,0:T(8,128)} %get-tuple-element.14.w_ref, f32[4096,512]{1,0:T(8,128)} %v_ref.7, f32[3,512,512]{2,1,0:T(8,128)} %get-tuple-element.15.vc_ref, ...), custom_call_target="tpu_custom_call", output_to_operand_aliasing={{}: (7, {})} | custom-call | flops 12884901888 | bytes 33554432 | tf_op jit(solution)/shard_map/finish_chunk/pallas_call | solution.py:611
  280.0 0.0 collective-permute-done.1
  280.0 1.4 add.37
  281.5 1.5 collective-permute-start.3
  283.0 22.0 %finish_chunk.7 = f32[4096,2048]{1,0:T(8,128)} custom-call(s32[9]{0:T(128)} %get-tuple-element.29.order_ref, f32[4096,2048]{1,0:T(8,128)} %a_ref.7, f32[4096,512]{1,0:T(8,128)} %get-tuple-element.14.w_ref, f32[4096,512]{1,0:T(8,128)} %v_ref.7, f32[3,512,512]{2,1,0:T(8,128)} %get-tuple-element.15.vc_ref, ...), custom_call_target="tpu_custom_call", output_to_operand_aliasing={{}: (7, {})} | custom-call | flops 12884901888 | bytes 33554432 | tf_op jit(solution)/shard_map/finish_chunk/pallas_call | solution.py:611
  305.0 6.3 %collective-permute-done.3 = f32[512,512]{1,0:T(8,128)} collective-permute-done((f32[512,512]{1,0:T(8,128)S(1)}, f32[512,512]{1,0:T(8,128)}, u32[]{:S(2)}, u32[]{:S(2)}) %collective-permute-start.3) | collective-permute-done | bytes 1048608 | tf_op jit(solution)/shard_map/ppermute | solution.py:636
  311.3 1.4 broadcast_select_fusion
  312.7 1.0 fusion.8
  313.7 14.0 %convolution_subtract_fusion = f32[512,4096]{1,0:T(8,128)} fusion(f32[512,4096]{1,0:T(8,128)} %b_hbm.1, f32[512,512]{1,0:T(8,128)S(1)} %fusion.8, f32[4096,512]{1,0:T(8,128)} %v_ref.7), kind=kOutput, calls=%fused_computation | convolution fusion | flops 6444548096 | bytes 26214400 | tf_op jit(solution)/shard_map/dot_general | solution.py:112
  (1 shorter events, 0.0 us)
Async XLA Ops:
  2.9 200.3 %copy-start = (f32[512,512]{1,0:T(8,128)S(1)}, f32[512,512]{1,0:T(8,128)}, u32[]{:S(2)}) copy-start(f32[512,512]{1,0:T(8,128)} %t_ref.1) | copy-start | bytes 3145732
  192.8 59.5 %collective-permute-start = (f32[512,512]{1,0:T(8,128)}, f32[512,512]{1,0:T(8,128)}, u32[]{:S(2)}, u32[]{:S(2)}) collective-permute-start(f32[512,512]{1,0:T(8,128)} %get-tuple-element.18), channel_id=1, source_target_pairs={{0,8},{24,16},{1,9},{25,17},{2,10},{26,18},{3,11},{27,19},{4,12},{... | collective-permute-start | bytes 3145736 | tf_op jit(solution)/shard_map/ppermute | solution.py:636
  199.4 55.9 %collective-permute-start.2 = (f32[512,512]{1,0:T(8,128)}, f32[512,512]{1,0:T(8,128)}, u32[]{:S(2)}, u32[]{:S(2)}) collective-permute-start(f32[512,512]{1,0:T(8,128)} %slice_bitcast_fusion), channel_id=1, source_target_pairs={{16,24},{8,0},{17,25},{9,1},{18,26},{10,2},{19,27},{11,3},{20,28},... | collective-permute-start | bytes 3145736 | tf_op jit(solution)/shard_map/ppermute | solution.py:636
  230.1 22.1 %copy-start.1 = (f32[512,512]{1,0:T(8,128)S(1)}, f32[512,512]{1,0:T(8,128)}, u32[]{:S(2)}) copy-start(f32[512,512]{1,0:T(8,128)} %get-tuple-element.18) | copy-start | bytes 3145732
  253.7 26.4 %collective-permute-start.1 = (f32[512,512]{1,0:T(8,128)S(1)}, f32[512,512]{1,0:T(8,128)}, u32[]{:S(2)}, u32[]{:S(2)}) collective-permute-start(f32[512,512]{1,0:T(8,128)S(1)} %add.36), channel_id=1, source_target_pairs={{8,16},{16,8},{9,17},{17,9},{10,18},{18,10},{11,19},{19,11},{12,20... | collective-permute-start | bytes 3145736 | tf_op jit(solution)/shard_map/ppermute | solution.py:636
  281.5 29.8 %collective-permute-start.3 = (f32[512,512]{1,0:T(8,128)S(1)}, f32[512,512]{1,0:T(8,128)}, u32[]{:S(2)}, u32[]{:S(2)}) collective-permute-start(f32[512,512]{1,0:T(8,128)S(1)} %add.37), channel_id=1, source_target_pairs={{16,24},{8,0},{17,25},{9,1},{18,26},{10,2},{19,27},{11,3},{20,28},... | collective-permute-start | bytes 3145736 | tf_op jit(solution)/shard_map/ppermute | solution.py:636
where the time goes:
time: 328 us
  Pallas kernels  278 us (85%)
  matrix products  19.3 us (6%)
  starting transfers between devices  9.02 us (3%)
  other arithmetic  7.69 us (2%)
  local copies, waits for them, and re-layouts  6.83 us (2%)
  waiting for transfers between devices  6.29 us (2%)
    pallas_call x1, Pallas kernels, front(): pl.pallas_call(front_kernel, out_shape=[shape(3, *chunk), shape(3, *chunk...  190 us
    pallas_call x4, Pallas kernels, finish_chunk(): pl.pallas_call(finish_kernel, out_shape=jax.ShapeDtypeStruct(matrix.shape...  88.1 us
    dot_general x4, matrix products, dot(): jnp.dot(a, b, precision=lax.Precision.HIGH, preferred_element_type=jnp.fl...  19.3 us
    ppermute x4, starting transfers between devices, send(): return lax.ppermute(x, 'row', pairs)  9.02 us
  transfers between devices with their start and end apart: 4, of which 1 were waited for; matrix products, arithmetic and copies ran while one was open for 4% of the time, Pallas kernels for 27%

commit v1 on v0

--- a/solution.py
+++ b/solution.py
@@ -1,3 +1,5 @@
+import functools
+
 import jax
 import jax.numpy as jnp
 from jax import lax
@@ -207,7 +209,7 @@
 
 
 MESH = pl.DeviceIdType.MESH
-INNER, FINAL, OUTER = [(1, 2), (2, 1)], [(2, 3), (1, 0)], [(0, 1), (3, 2)]
+INNER, FINAL = [(1, 2), (2, 1)], [(2, 3), (1, 0)]
 
 
 def triple(a, b, dims):
@@ -224,10 +226,10 @@
 
 def front_kernel(
     a_hbm, v_hbm, own_hbm, b_hbm, t_ref,
-    v_all, w_all, w_rows, q_out, cross_out,
-    a_buf, b_buf, v_buf, own, part, outer_in, inner_in, final_in, w_own, q_acc, total,
+    v_all, w_all, w_rows, q_out, y_out,
+    a_buf, b_buf, v_buf, own, part, outer_in, inner_in, final_in, w_own, q_acc, q_in, total, cross, slots,
     half_in, quarter_in, eighth_in, line_in, far_in,
-    a_sem, b_sem, v_sem, local_sem, send_sem, recv_sem,
+    a_sem, b_sem, v_sem, slot_sem, local_sem, send_sem, recv_sem,
 ):
     z, col, y = (lax.axis_index(name) for name in ("row", "col", "grp"))
     core, x = lax.rem(col, 2), lax.div(col, 2)
@@ -236,6 +238,7 @@
     steps = v_buf.shape[0] // tile
     low = z < 2
     edge = (z == 0) | (z == 3)
+    inside = jnp.logical_not(edge)
     near = jnp.where(low, 1, 2)
     outward = jnp.where(low, 0, 3)
     across = jnp.where(low, 2, 1)
@@ -290,7 +293,7 @@
     def _():
         gather_v["in"].start()
 
-    @pl.when(jnp.logical_not(edge))
+    @pl.when(inside)
     def _():
         gather_v["over"].start()
         gather_v["out"].start()
@@ -305,6 +308,8 @@
     outer = [remote(12 + i, part.at[i], outer_in.at[i], along(near)) for i in range(3)]
     inner = [remote(15 + i, outer_in.at[i], inner_in.at[i], along(across)) for i in range(2)]
     final = remote(17, inner_in.at[0], final_in, along(outward))
+    pass_q = remote(39, q_acc, q_in, along(near))
+    fetch_slots = [pltpu.make_async_copy(v_all.at[i], slots.at[i], slot_sem.at[i]) for i in range(3)]
 
     def product(i):
         def body(step, carry):
@@ -344,62 +349,99 @@
             outer[i].start()
 
         if i == 1:
-            @pl.when(jnp.logical_not(edge))
+            @pl.when(inside)
             def _():
                 gather_v["over"].wait_recv()
                 gather_v["out2"].start()
                 gather_v["in"].wait_recv()
                 gather_v["over2"].start()
 
-    @pl.when(jnp.logical_not(edge))
+    @pl.when(inside)
     def _():
         outer[0].wait_recv()
         outer_in[0] += part[0]
         inner[0].start()
+        gather_v["over2"].wait_recv()
+        gather_v["out3"].start()
+        for copy in fetch_slots:
+            copy.start()
 
     fetch_b(0, 0).start()
     product(3)
-
-    @pl.when(jnp.logical_not(edge))
-    def _():
-        gather_v["over2"].wait_recv()
-        gather_v["out3"].start()
+    fetch_own.wait()
+    total[...] = triple(own[...], part[3], ((0,), (0,)))
+
+    def project_b(step, carry):
+        slot = lax.rem(step, 2)
+
+        @pl.when(step < steps - 1)
+        def _():
+            fetch_b(step + 1, 1 - slot).start()
+
+        fetch_b(step, slot).wait()
+        rows = pl.ds(pl.multiple_of(step * tile, tile), tile)
+        value = triple(b_buf[slot], v_buf[rows, :], ((1,), (0,)))
+
+        @pl.when(step == 0)
+        def _():
+            q_acc[...] = value
+
+        @pl.when(step > 0)
+        def _():
+            q_acc[...] += value
+
+        return carry
+
+    lax.fori_loop(0, steps // 2, project_b, 0)
+
+    @pl.when(inside)
+    def _():
         outer[1].wait_recv()
         outer_in[1] += part[1]
         inner[1].start()
-
-    def project_b(step, carry):
-        slot = lax.rem(step, 2)
-
-        @pl.when(step < steps - 1)
-        def _():
-            fetch_b(step + 1, 1 - slot).start()
-
-        fetch_b(step, slot).wait()
-        rows = pl.ds(pl.multiple_of(step * tile, tile), tile)
-        value = triple(b_buf[slot], v_buf[rows, :], ((1,), (0,)))
-
-        @pl.when(step == 0)
-        def _():
-            q_acc[...] = value
-
-        @pl.when(step > 0)
-        def _():
-            q_acc[...] += value
-
-        return carry
-
-    @pl.when(jnp.logical_not(edge))
-    def _():
         inner[0].wait_recv()
         inner_in[0] += part[2]
         final.start()
 
-    lax.fori_loop(0, steps, project_b, 0)
-    put_q = pltpu.make_async_copy(q_acc, q_out, local_sem.at[1])
-    put_q.start()
-
-    @pl.when(jnp.logical_not(edge))
+    @pl.when(edge)
+    def _():
+        for name in ("out", "out2", "out3"):
+            gather_v[name].wait_recv()
+        for copy in fetch_slots:
+            copy.start()
+
+    for copy in fetch_slots:
+        copy.wait()
+    total[...] += triple(slots[2], part[0], ((0,), (0,)))
+    total[...] += triple(slots[jnp.where(edge, 0, 1)], part[2], ((0,), (0,)))
+    total[...] += triple(slots[jnp.where(edge, 1, 0)], part[1], ((0,), (0,)))
+
+    def piece(start, size):
+        return pl.ds(pl.multiple_of(start, size), size)
+
+    sizes = [depth // 2, depth // 4, depth // 8]
+    bits, targets, landings = [core, x, y], [by_core, by_x, by_y], [half_in, quarter_in, eighth_in]
+    base = 0
+    reduces = []
+    for i in range(3):
+        other = base + (1 - bits[i]) * sizes[i]
+        base = base + bits[i] * sizes[i]
+        copy = remote(31 + i, total.at[piece(other, sizes[i])], landings[i], targets[i])
+        copy.start()
+        if i == 0:
+            lax.fori_loop(steps // 2, steps, project_b, 0)
+        copy.wait_recv()
+        here = piece(base, sizes[i])
+        total[here, :] += landings[i][...]
+        reduces.append(copy)
+    mine = piece(base, sizes[2])
+    line = [
+        remote(34, total.at[mine], line_in, along(beside)),
+        remote(35, eighth_in, far_in, along(lax.rem(z + 2, 4))),
+    ]
+    line[0].start()
+
+    @pl.when(inside)
     def _():
         inner[1].wait_recv()
         part[3] += inner_in[1]
@@ -428,46 +470,9 @@
     for slot, (side, i) in enumerate([(0, 1), (1, 2), (0, 2), (1, 1), (0, 3), (1, 3)]):
         shares.append(remote(25 + slot, w_rows.at[places[side][i]], w_rows.at[places[side][4 + i]], by_core))
 
-    for hop in hops[:2]:
+    for hop in hops[:3]:
         hop.start()
-
-    total[...] = triple(own_value(fetch_own, own), part[3], ((0,), (0,)))
-
-    def piece(start, size):
-        return pl.ds(pl.multiple_of(start, size), size)
-
-    sizes = [depth // 2, depth // 4, depth // 8]
-    bits, targets, landings = [core, x, y], [by_core, by_x, by_y], [half_in, quarter_in, eighth_in]
-    base = 0
-    reduces = []
-    for i in range(3):
-        other = base + (1 - bits[i]) * sizes[i]
-        base = base + bits[i] * sizes[i]
-        copy = remote(31 + i, total.at[piece(other, sizes[i])], landings[i], targets[i])
-        copy.start()
-        copy.wait_recv()
-        here = piece(base, sizes[i])
-        total[here, :] += landings[i][...]
-        reduces.append(copy)
-    mine = piece(base, sizes[2])
-    line = [
-        remote(34, total.at[mine], line_in, along(beside)),
-        remote(35, eighth_in, far_in, along(lax.rem(z + 2, 4))),
-    ]
-    line[0].start()
-
-    @pl.when(edge)
-    def _():
-        gather_w["in"].start()
-
-    @pl.when(jnp.logical_not(edge))
-    def _():
-        gather_w["over"].start()
-        gather_w["out"].start()
-
     shares[0].start()
-    hops[2].start()
-    hops[3].start()
     put_w = pltpu.make_async_copy(w_own, w_rows.at[pl.ds(0, depth)], local_sem.at[2])
     put_w.start()
 
@@ -475,40 +480,71 @@
     eighth_in[...] = total[mine, :] + line_in[...]
     line[1].start()
 
+    @pl.when(edge)
+    def _():
+        gather_w["in"].start()
+        pass_q.start()
+
+    @pl.when(inside)
+    def _():
+        gather_w["over"].start()
+        gather_w["out"].start()
+
+    line[1].wait()
+    cross[mine, :] = eighth_in[...] + far_in[...]
+    returns = []
+    for i in (2, 1, 0):
+        here = piece(base - lax.rem(base, sizes[i]), sizes[i])
+        returns.append(remote(36 + i, cross.at[here], cross.at[here], targets[i]))
+    returns[0].start()
+    hops[3].start()
+    returns[0].wait_recv()
+    returns[1].start()
     for i in range(2):
         hops[i].wait_recv()
         hops[4 + i].start()
         shares[1 + i].start()
-
-    line[1].wait()
-    eighth_in[...] += far_in[...]
-    put_c = pltpu.make_async_copy(eighth_in, cross_out.at[mine], local_sem.at[3])
-    put_c.start()
-    put_c.wait()
-    returns = []
-    for i in (2, 1, 0):
-        here = piece(base - lax.rem(base, sizes[i]), sizes[i])
-        copy = remote(36 + i, cross_out.at[here], cross_out.at[here], targets[i])
-        copy.start()
-        copy.wait_recv()
-        returns.append(copy)
-
-    @pl.when(jnp.logical_not(edge))
+    returns[1].wait_recv()
+    returns[2].start()
+
+    @pl.when(inside)
     def _():
         gather_w["over"].wait_recv()
         gather_w["out2"].start()
         gather_w["in"].wait_recv()
         gather_w["over2"].start()
 
-    for i in range(2, 6):
+    for i in range(2, 4):
         hops[i].wait_recv()
         shares[1 + i].start()
-    for copy in hops + shares + reduces + returns:
+    returns[2].wait()
+    far_product = triple(cross[...], t_ref[...], ((1,), (0,)))
+    own[...] = triple(t_ref[...], far_product, ((0,), (0,)))
+    put_y = pltpu.make_async_copy(own, y_out, local_sem.at[3])
+    put_y.start()
+    for i in range(4, 6):
+        hops[i].wait_recv()
+        shares[1 + i].start()
+
+    @pl.when(inside)
+    def _():
+        pass_q.wait_recv()
+        q_acc[...] += q_in[...]
+
+    put_q = pltpu.make_async_copy(q_acc, q_out, local_sem.at[1])
+
+    @pl.when(edge)
+    def _():
+        pass_q.wait_send()
+
+    put_q.start()
+    for copy in hops + shares + reduces + returns[:2]:
         copy.wait_send()
     for copy in shares:
         copy.wait_recv()
     put_w.wait()
     put_q.wait()
+    put_y.wait()
 
     @pl.when(edge)
     def _():
@@ -516,12 +552,10 @@
         gather_w["in"].wait_send()
         for copy in outer:
             copy.wait_send()
-        for name in ("out", "out2", "out3"):
-            gather_v[name].wait_recv()
         for name in ("out", "out2"):
             gather_w[name].wait_recv()
 
-    @pl.when(jnp.logical_not(edge))
+    @pl.when(inside)
     def _():
         for name in ("over", "out", "out2", "over2", "out3"):
             gather_v[name].wait_send()
@@ -530,11 +564,6 @@
         for copy in inner + [final]:
             copy.wait_send()
         gather_w["over2"].wait_recv()
-
-
-def own_value(fetch, own):
-    fetch.wait()
-    return own[...]
 
 
 def front(matrix, reflectors, own_v, basis_rows, tfactor):
@@ -558,10 +587,12 @@
         scratch_shapes=[
             vmem(2, tile, depth), vmem(2, depth, tile), vmem(rows, wide), vmem(*chunk), vmem(4, *chunk),
             vmem(3, *chunk), vmem(2, *chunk), vmem(*chunk), vmem(*chunk), vmem(*chunk), vmem(*chunk),
+            vmem(*chunk), vmem(*chunk), vmem(3, *chunk),
             vmem(depth // 2, wide), vmem(depth // 4, wide), vmem(depth // 8, wide), vmem(depth // 8, wide),
             vmem(depth // 8, wide),
             pltpu.SemaphoreType.DMA((2,)), pltpu.SemaphoreType.DMA((2,)), pltpu.SemaphoreType.DMA((4,)),
-            pltpu.SemaphoreType.DMA((4,)), pltpu.SemaphoreType.DMA((39,)), pltpu.SemaphoreType.DMA((39,)),
+            pltpu.SemaphoreType.DMA((3,)), pltpu.SemaphoreType.DMA((4,)), pltpu.SemaphoreType.DMA((40,)),
+            pltpu.SemaphoreType.DMA((40,)),
         ],
         compiler_params=pltpu.CompilerParams(
             collective_id=0, has_side_effects=True, vmem_limit_bytes=60 * 1024 * 1024
@@ -573,63 +604,82 @@
     )(matrix, reflectors, own_v, basis_rows, tfactor)
 
 
-def finish_kernel(order_ref, a_ref, w_ref, v_ref, vc_ref, wc_ref, y_ref, *rest):
-    out_ref, right = rest[-2:]
-
-    @pl.when(pl.program_id(0) == 0)
-    def _():
-        chunk = vc_ref[...]
-        z_high, z_low = halves(wc_ref[...] - triple(chunk, y_ref[...], ((1,), (1,))))
-        v_high, v_low = halves(chunk)
-        right[...] = jnp.concatenate([v_high, v_high, v_low, z_high, z_high, z_low], axis=1)
-
-    w_high, w_low = halves(w_ref[...])
-    v_high, v_low = halves(v_ref[...])
-    left = jnp.concatenate([w_high, w_low, w_high, v_high, v_low, v_high], axis=1)
+def finish_kernel(wide_calls, order_ref, a_ref, w_ref, v_ref, y_ref, *rest):
+    (*chunks, out_ref, left, right), count = rest, wide_calls
+    first = (pl.program_id(0) == 0) & (pl.program_id(1) == 0)
+
+    @pl.when(first)
+    def _():
+        for i in range(count):
+            v_chunk = chunks[2 * i][...]
+            w_chunk = chunks[2 * i + 1][...]
+            if len(chunks) % 2 == 1 and count == 1:
+                w_chunk = jnp.where(order_ref[1] > 0, chunks[2][...], w_chunk)
+            z_high, z_low = halves(w_chunk - triple(v_chunk, y_ref[...], ((1,), (1,))))
+            v_high, v_low = halves(v_chunk)
+            right[i] = jnp.concatenate([v_high, v_high, v_low, z_high, z_high, z_low], axis=1)
+
+    @pl.when(pl.program_id(1) == 0)
+    def _():
+        w_high, w_low = halves(w_ref[...])
+        v_high, v_low = halves(v_ref[...])
+        left[...] = jnp.concatenate([w_high, w_low, w_high, v_high, v_low, v_high], axis=1)
+
     out_ref[...] = a_ref[...] - lax.dot_general(
-        left, right[...], (((1,), (1,)), ((), ())), preferred_element_type=jnp.float32
+        left[...], right[pl.program_id(1)], (((1,), (1,)), ((), ())), preferred_element_type=jnp.float32
     )
 
 
-def finish_chunk(matrix, w_rows, v_row, v_chunks, w_chunks, slots, inner, order, out):
-    rows, (depth, wide) = matrix.shape[0], v_chunks.shape[1:]
-    tile, steps = depth, rows // depth
+def finish(matrix, w_rows, v_row, inner, owners, flag, tiles, chunks, out):
+    rows, wide = v_row.shape
+    depth = inner.shape[0]
+    count, steps = owners.shape[0], tiles.shape[0]
+    tile, lead = rows // steps, count + 1
+    order = jnp.concatenate([owners, flag, tiles]).astype(jnp.int32)
     specs = [
-        pl.BlockSpec((tile, depth), lambda i, c: (c[i + 1], c[0])),
-        pl.BlockSpec((tile, wide), lambda i, c: (i, 0)),
-        pl.BlockSpec((tile, wide), lambda i, c: (c[i + 1], 0)),
-        pl.BlockSpec((None, depth, wide), lambda i, c: (slots[0], 0, 0)),
-        pl.BlockSpec((None, depth, wide), lambda i, c: (slots[1], 0, 0)),
-        pl.BlockSpec(inner.shape, lambda i, c: (0, 0)),
+        pl.BlockSpec((tile, depth), lambda i, j, c: (c[i + lead], c[j])),
+        pl.BlockSpec((tile, wide), lambda i, j, c: (i, 0)),
+        pl.BlockSpec((tile, wide), lambda i, j, c: (c[i + lead], 0)),
+        pl.BlockSpec(inner.shape, lambda i, j, c: (0, 0)),
     ]
-    args = [matrix, w_rows, v_row, v_chunks, w_chunks, inner]
-    alias = {}
+    args = [matrix, w_rows, v_row, inner]
+    for array, slot in chunks:
+        if array.ndim == 3:
+            specs.append(pl.BlockSpec((None, depth, wide), lambda i, j, c, at=slot: (at, 0, 0)))
+        else:
+            specs.append(pl.BlockSpec((depth, wide), lambda i, j, c, at=slot: (at, 0)))
+        args.append(array)
+    kernel, alias = functools.partial(finish_kernel, count), {}
     if out is not None:
         specs.append(pl.BlockSpec(memory_space=pl.ANY))
         args.append(out)
-        alias = {7: 0}
+        alias = {len(args): 0}
+        inside = kernel
+
+        def kernel(*refs):
+            inside(*refs[: len(args)], *refs[len(args) + 1 :])
+
     return pl.pallas_call(
-        finish_kernel,
+        kernel,
         out_shape=jax.ShapeDtypeStruct(matrix.shape, jnp.float32),
         grid_spec=pltpu.PrefetchScalarGridSpec(
             num_scalar_prefetch=1,
-            grid=(steps,),
+            grid=(steps, count),
             in_specs=specs,
-            out_specs=pl.BlockSpec((tile, depth), lambda i, c: (c[i + 1], c[0])),
-            scratch_shapes=[pltpu.VMEM((depth, 6 * wide), jnp.bfloat16)],
+            out_specs=pl.BlockSpec((tile, depth), lambda i, j, c: (c[i + lead], c[j])),
+            scratch_shapes=[
+                pltpu.VMEM((tile, 6 * wide), jnp.bfloat16),
+                pltpu.VMEM((count, depth, 6 * wide), jnp.bfloat16),
+            ],
         ),
         input_output_aliases=alias,
         cost_estimate=pl.CostEstimate(
-            flops=12 * rows * depth * wide,
-            bytes_accessed=8 * rows * (depth + wide),
+            flops=12 * rows * depth * wide * count,
+            bytes_accessed=8 * rows * (depth * count + wide),
             transcendentals=0,
         ),
-        name="finish_chunk",
+        name="finish",
     )(order, *args)
-
-
-def scalar(x):
-    return x.astype(jnp.int32).reshape(1)
 
 
 def send(x, pairs):
@@ -641,39 +691,30 @@
     member, groups = lax.axis_index(("col", "grp")), lax.axis_size(("col", "grp"))
     depth = reflectors.shape[0] // groups
     own_v = lax.dynamic_slice_in_dim(reflectors, member * depth, depth, 0)
-    v_all, w_all, w_rows, q_proj, cross = front(matrix, reflectors, own_v, basis_rows, tfactor)
-    inner = dot(tfactor.T, dot(cross, tfactor))
+    v_all, w_all, w_rows, q_pair, inner = front(matrix, reflectors, own_v, basis_rows, tfactor)
 
     bits = jnp.arange(8)
     tiles = (col ^ (2 * (bits // 2 % 2) + bits // 4)) * 2 + (y ^ (bits % 2))
     edge, low = (z == 0) | (z == 3), z < 2
-    owners = [
+    owners = jnp.stack([
         z,
         jnp.where(edge, jnp.where(low, 1, 2), jnp.where(low, 2, 1)),
         jnp.where(edge, jnp.where(low, 2, 1), jnp.where(low, 0, 3)),
         jnp.where(low, 3, 0),
-    ]
-    w_third = w_all[2]
-    w_last = jnp.where(edge, send(w_third, FINAL), w_third)
-    q_pair = q_proj + send(q_proj, OUTER)
-
-    out = None
-    for i, owner in enumerate(owners):
-        order = jnp.concatenate([scalar(owner), tiles.astype(jnp.int32)])
-        if i == 2:
-            out, q_pair = lax.optimization_barrier((out, q_pair))
-            q_full = q_pair + send(q_pair, INNER)
-        if i == 3:
-            out, q_full, w_last = lax.optimization_barrier((out, q_full, w_last))
-            q_full = jnp.where(edge, send(q_full, FINAL), q_full)
-        v_from, w_from, slots = v_all, w_all, (i - 1, i - 1)
-        if i == 0:
-            v_from, w_from, slots = own_v[None], w_rows.reshape(groups, depth, -1), (0, 0)
-        if i == 3:
-            w_from, slots = w_last[None], (2, 0)
-        out = finish_chunk(matrix, w_rows, reflectors, v_from, w_from, slots, inner, order, out)
-
-    out, q_full = lax.optimization_barrier((out, q_full))
+    ])
+    flag = edge.astype(jnp.int32).reshape(1)
+    w_last = send(w_all[2], FINAL)
+    q_full = q_pair + send(q_pair, INNER)
+
+    chunks = [(own_v, 0), (w_rows, 0), (v_all, 0), (w_all, 0), (v_all, 1), (w_all, 1)]
+    out = finish(matrix, w_rows, reflectors, inner, owners[:3], flag, tiles, chunks, None)
+    out, w_last, q_full = lax.optimization_barrier((out, w_last, q_full))
+    q_last = send(q_full, FINAL)
+    chunks = [(v_all, 2), (w_all, 2), (w_last, 0)]
+    out = finish(matrix, w_rows, reflectors, inner, owners[3:], flag, tiles, chunks, out)
+
+    out, q_full, q_last = lax.optimization_barrier((out, q_full, q_last))
+    q_full = jnp.where(edge, q_last, q_full)
     new_basis = basis_rows - dot(dot(q_full, tfactor), reflectors.T)
     return (out, new_basis)
 

time: 328 us -> 267 us (0.81)
  Pallas kernels: 278 us -> 235 us
  other arithmetic: 7.69 us -> 2 us
  starting transfers between devices: 9.02 us -> 4.63 us
  waiting for transfers between devices: 6.29 us -> 2.99 us
    pallas_call x1, Pallas kernels: 190 us -> 154 us  [front(): pl.pallas_call(front_kernel, out_shape=[shape(3, *chunk), shape(3, *chunk...]
    pallas_call x4 -> x2, Pallas kernels: 88.1 us -> 81 us  [finish(): pl.pallas_call(kernel, out_shape=jax.ShapeDtypeStruct(matrix.shape, jnp.f...]
    ppermute x4 -> x3, starting transfers between devices: 9.02 us -> 4.63 us  [send(): return lax.ppermute(x, 'row', pairs)]
    select_n x2 -> x0, other arithmetic: 4.15 us -> none  [the longest x1 2.72 us: line_step(): w_last = jnp.where(edge, send(w_third, FINAL), w_third)]
    ppermute x4 -> x3, waiting for transfers between devices: 6.29 us -> 2.99 us  [send(): return lax.ppermute(x, 'row', pairs)]
    dot_general x4 -> x2, matrix products: 19.3 us -> 16.3 us  [dot(): jnp.dot(a, b, precision=lax.Precision.HIGH, preferred_element_type=jnp.fl...]
  transfers between devices with their start and end apart: 4 -> 3, of which waited for: 1 -> 1; matrix products, arithmetic and copies ran while one was open for 4% -> 1% of each run, Pallas kernels for 27% -> 30%
where the time goes in v1:
time: 267 us
  Pallas kernels  235 us (88%)
  matrix products  16.3 us (6%)
  local copies, waits for them, and re-layouts  5.22 us (2%)
  starting transfers between devices  4.63 us (2%)
  waiting for transfers between devices  2.99 us (1%)
    pallas_call x1, Pallas kernels, front(): pl.pallas_call(front_kernel, out_shape=[shape(3, *chunk), shape(3, *chunk...  154 us
    pallas_call x2, Pallas kernels, finish(): pl.pallas_call(kernel, out_shape=jax.ShapeDtypeStruct(matrix.shape, jnp.f...  81 us
    dot_general x2, matrix products, dot(): jnp.dot(a, b, precision=lax.Precision.HIGH, preferred_element_type=jnp.fl...  16.3 us
  transfers between devices with their start and end apart: 3, of which 1 were waited for; matrix products, arithmetic and copies ran while one was open for 1% of the time, Pallas kernels for 30%

profile of v1, /device:TPU:0, one launch (start us, length us, event | category | flops | bytes accessed | tf_op | source)
XLA Modules:
  0.0 266.7 jit_solution(2011130101432959161)
XLA Ops:
  0.6 2.3 constant_dynamic-slice_fusion.own_hbm.rest_0_
  2.9 153.9 %front.1 = (f32[3,512,512]{2,1,0:T(8,128)}, f32[3,512,512]{2,1,0:T(8,128)}, f32[4096,512]{1,0:T(8,128)}, f32[512,512]{1,0:T(8,128)}, f32[512,512]{1,0:T(8,128)}) custom-call(f32[4096,2048]{1,0:T(8,128)} %refs_1_.1, f32[4096,512]{1,0:T(8,128)} %refs_3_.1, f32[512,512]{1,0:T(8,128)} %constant_dynamic-slice_fusion.own_hbm.rest_0_, f32[512,4096]{1,0:T(8,128)} %b_hbm.1, ...), custom_call_target="tpu_custom_call" | custom-call | flops 32212254720 | bytes 41943040 | tf_op jit(solution)/shard_map/front/pallas_call | solution.py:582
  156.8 2.3 slice_bitcast_fusion
  159.0 1.3 collective-permute-start
  160.3 1.7 collective-permute-start.1
  162.0 0.7 concatenate.7.order_ref
  162.7 0.0 copy-start.2
  162.7 58.7 %finish.2.refs_8_ = f32[4096,2048]{1,0:T(8,128)} custom-call(s32[12]{0:T(128)} %concatenate.7.order_ref, f32[4096,2048]{1,0:T(8,128)} %refs_1_.1, f32[4096,512]{1,0:T(8,128)} %get-tuple-element.13.w_ref.rest_1_.refs_2_, f32[4096,512]{1,0:T(8,128)} %refs_3_.1, f32[512,512]{1,0:T(8,128)} %get-tuple-element.14.y_ref.refs_4_, ...), custom_call_target="tpu_custom_call" | custom-call | flops 38654705664 | bytes 67108864 | tf_op jit(solution)/shard_map/finish/pallas_call | solution.py:662
  221.4 0.6 pad_add_fusion.refs_0_
  221.9 0.0 collective-permute-done.1
  221.9 0.0 copy-done.2
  221.9 1.4 add.33
  223.4 0.0 copy-start.1
  223.4 0.0 collective-permute-done.refs_7_
  223.4 0.0 copy-start
  223.4 1.6 collective-permute-start.2
  225.1 0.0 copy-done
  225.1 22.3 %finish.3 = f32[4096,2048]{1,0:T(8,128)} custom-call(s32[10]{0:T(128)} %pad_add_fusion.refs_0_, f32[4096,2048]{1,0:T(8,128)} %refs_1_.1, f32[4096,512]{1,0:T(8,128)} %get-tuple-element.13.w_ref.rest_1_.refs_2_, f32[4096,512]{1,0:T(8,128)} %refs_3_.1, f32[512,512]{1,0:T(8,128)} %get-tuple-element.14.y_ref.refs_4_, ...), custom_call_target="tpu_custom_call", output_to_operand_aliasing={{}: (8, {})} | custom-call | flops 12884901888 | bytes 33554432 | tf_op jit(solution)/shard_map/finish/pallas_call | solution.py:662
  247.4 3.0 %collective-permute-done.2 = f32[512,512]{1,0:T(8,128)} collective-permute-done((f32[512,512]{1,0:T(8,128)S(1)}, f32[512,512]{1,0:T(8,128)}, u32[]{:S(2)}, u32[]{:S(2)}) %collective-permute-start.2) | collective-permute-done | bytes 1048608 | tf_op jit(solution)/shard_map/ppermute | solution.py:686
  250.4 0.0 copy-done.1
  250.4 2.2 fusion
  252.6 14.0 %convolution_subtract_fusion = f32[512,4096]{1,0:T(8,128)} fusion(f32[512,4096]{1,0:T(8,128)} %b_hbm.1, f32[512,512]{1,0:T(8,128)S(1)} %fusion, f32[4096,512]{1,0:T(8,128)} %refs_3_.1), kind=kOutput, calls=%fused_computation | convolution fusion | flops 6444548096 | bytes 26214400 | tf_op jit(solution)/shard_map/dot_general | solution.py:114
  (1 shorter events, 0.0 us)
Async XLA Ops:
  159.0 64.3 %collective-permute-start = (f32[512,512]{1,0:T(8,128)}, f32[512,512]{1,0:T(8,128)S(1)}, u32[]{:S(2)}, u32[]{:S(2)}) collective-permute-start(f32[512,512]{1,0:T(8,128)} %slice_bitcast_fusion), channel_id=1, source_target_pairs={{16,24},{8,0},{17,25},{9,1},{18,26},{10,2},{19,27},{11,3},{20,28},... | collective-permute-start | bytes 3145736 | tf_op jit(solution)/shard_map/ppermute | solution.py:686
  160.3 61.6 %collective-permute-start.1 = (f32[512,512]{1,0:T(8,128)}, f32[512,512]{1,0:T(8,128)}, u32[]{:S(2)}, u32[]{:S(2)}) collective-permute-start(f32[512,512]{1,0:T(8,128)} %get-tuple-element.17), channel_id=1, source_target_pairs={{8,16},{16,8},{9,17},{17,9},{10,18},{18,10},{11,19},{19,11},{12,20... | collective-permute-start | bytes 3145736 | tf_op jit(solution)/shard_map/ppermute | solution.py:686
  162.7 59.2 %copy-start.2 = (f32[512,512]{1,0:T(8,128)S(1)}, f32[512,512]{1,0:T(8,128)}, u32[]{:S(2)}) copy-start(f32[512,512]{1,0:T(8,128)} %get-tuple-element.17) | copy-start | bytes 3145732
  223.4 27.0 %copy-start.1 = (f32[512,512]{1,0:T(8,128)S(1)}, f32[512,512]{1,0:T(8,128)}, u32[]{:S(2)}) copy-start(f32[512,512]{1,0:T(8,128)} %t_ref.1) | copy-start | bytes 3145732
  223.4 1.7 copy-start
  223.4 27.0 %collective-permute-start.2 = (f32[512,512]{1,0:T(8,128)S(1)}, f32[512,512]{1,0:T(8,128)}, u32[]{:S(2)}, u32[]{:S(2)}) collective-permute-start(f32[512,512]{1,0:T(8,128)S(1)} %add.33), channel_id=1, source_target_pairs={{16,24},{8,0},{17,25},{9,1},{18,26},{10,2},{19,27},{11,3},{20,28},... | collective-permute-start | bytes 3145736 | tf_op jit(solution)/shard_map/ppermute | solution.py:686
